TPU v7x, 128 devices: a whole 4x4x4 slice. The times are simulated.
128 devices in a mesh: orb: 128 (over y, z, x, core).
Axes of the slice: x: 4, y: 4, z: 4, core: 2. Of those that a mesh axis runs over, the one named last changes fastest.
Arguments:
- orbitals: float32 [256, 48, 64, 128], P('orb'), may hold values from -6 to 6
- pair_list: int32 [128, 6, 2], P('orb'), may hold values from 0 to 255, as said below
- pair_count: int32 [128], P('orb'), may hold values from 1 to 6, 256 in all
- box_offset: int32 [256, 3], replicated, may hold values from 0 to 24
Outputs:
- exchange: float32 [256, 48, 64, 128], P('orb')
Inputs may be any that keep to these rules, and one draw needn't show every extreme that they name: `pair_list`: every orbital named in row d is owned by a device d - 1 to d + 1; the two orbitals of a pair differ; slot 0 of every row pairs with an orbital of a device exactly 1 away. `pair_count`: they sum to 256.
All inputs are finite; a program needn't handle non-finite values. No bound on the sum of `pair_count` on one device may be relied on, other than what follows from the above.
Results may differ from a plain program's by a relative error of at most 0.0003.
Values sent between devices are 32-bit elements; how exact they have to be, the bound alone decides.
No kernel may reach another device: no remote copies, remote signals or barrier semaphores. Data moves between devices by JAX's collectives and lax.ppermute only.
A program may use at most 128 MiB of HBM per device.

v0:
```python
import functools

import jax
import jax.numpy as jnp
import ml_dtypes
import numpy as np
from jax import lax
from jax.experimental import pallas as pl
from jax.experimental.pallas import tpu as pltpu
from jax.sharding import PartitionSpec as P

BOX_X, BOX_Y, BOX_Z = 48, 64, 128
BOX = (BOX_X, BOX_Y, BOX_Z)
ORB_DEV = 2
SLOTS = 6
TILES = BOX_Y // 8
PLANE = BOX_Y + 8
STENCIL_ROWS = (BOX_X + 2) * PLANE + 8
MARGIN = 24
WIDE = BOX_Y + MARGIN
SHIFT_PLANES = BOX_X + 2 * MARGIN + 1
SHIFT_ROWS = SHIFT_PLANES * WIDE
STENCIL_UNROLL = 8
BLOCK = 16
F32 = jnp.float32
BF16 = jnp.bfloat16


def sine_basis():
    k = np.arange(1, BOX_Z + 1)
    basis = np.sqrt(2.0 / (BOX_Z + 1)) * np.sin(np.pi * np.outer(k, k) / (BOX_Z + 1))
    high = basis.astype(np.float32).astype(ml_dtypes.bfloat16)
    low = (basis - high.astype(np.float64)).astype(ml_dtypes.bfloat16)
    half = np.concatenate([high, low], 1)
    weights = np.concatenate([half, half], 0)
    values = np.tile(2.0 * np.cos(np.pi * k / (BOX_Z + 1)), (8, 1)).astype(np.float32)
    return weights, values


def stencil_row(x):
    return pl.multiple_of(8 + (x + 1) * PLANE, 8)


def shift_row(x):
    return pl.multiple_of((x + MARGIN) * WIDE + MARGIN, 8)


def zero_rows(ref, first, rows):
    for k in range(rows // 8):
        ref[pl.ds(first + 8 * k, 8), :] = jnp.zeros((8, BOX_Z), F32)


def zero_margins(ref):
    def plane(p, _):
        row = pl.multiple_of(p * WIDE, 8)
        zero_rows(ref, row, MARGIN)

        @pl.when((p < MARGIN) | (p >= MARGIN + BOX_X))
        def _():
            zero_rows(ref, row + MARGIN, BOX_Y)

        return 0

    lax.fori_loop(0, SHIFT_PLANES, plane, 0)


def zero_borders(ref):
    zero_rows(ref, 0, 8 + PLANE)
    zero_rows(ref, STENCIL_ROWS - PLANE, PLANE)

    def plane(x, _):
        zero_rows(ref, pl.multiple_of(8 + (x + 1) * PLANE + BOX_Y, 8), 8)
        return 0

    lax.fori_loop(0, BOX_X, plane, 0)


def zero_box(ref):
    def plane(x, _):
        for t in range(TILES):
            ref[x, pl.ds(8 * t, 8), :] = jnp.zeros((8, BOX_Z), F32)
        return 0

    lax.fori_loop(0, BOX_X, plane, 0, unroll=2)


def sweep(source, target, centre, other=None, factor=None):
    def plane(x, carry):
        behind, here = carry
        row = stencil_row(x)
        ahead_row = stencil_row(x + 1)
        ahead = [source[pl.ds(ahead_row + 8 * t, 8), :] for t in range(TILES)]
        for t in range(TILES):
            above = source[pl.ds(row + 8 * t - 1, 8), :]
            below = source[pl.ds(row + 8 * t + 1, 8), :]
            total = (behind[t] + ahead[t]) + (above + below) + centre * here[t]
            if other is not None:
                total = total + factor * other[pl.ds(row + 8 * t, 8), :]
            target[pl.ds(row + 8 * t, 8), :] = total
        return here, ahead

    first = [source[pl.ds(stencil_row(-1) + 8 * t, 8), :] for t in range(TILES)]
    second = [source[pl.ds(stencil_row(0) + 8 * t, 8), :] for t in range(TILES)]
    lax.fori_loop(0, BOX_X, plane, (first, second), unroll=STENCIL_UNROLL)


def along_z(rows, weights):
    high = rows.astype(BF16)
    low = (rows - high.astype(F32)).astype(BF16)
    product = jnp.dot(
        jnp.concatenate([high, low], 1), weights[...], preferred_element_type=F32
    )
    return product[:, :BOX_Z] + product[:, BOX_Z:]


def solve_pair(lead, shift, partner, bufs, weights, values, gap, accum, lead_slot, partner_slot):
    gap_x, gap_y, gap_z = gap
    lane = lax.broadcasted_iota(jnp.int32, (8, BOX_Z), 1)
    one, two, three = bufs
    centre = values[...]

    inside = (lane >= gap_z) & (lane < BOX_Z + gap_z)
    turn = jnp.where(gap_z < 0, gap_z + BOX_Z, gap_z)

    def density_block(block, _):
        parts = []
        for q in range(BLOCK):
            x = block * BLOCK + q
            base = (x - gap_x + MARGIN) * WIDE + MARGIN - gap_y
            for t in range(TILES):
                value = shift[pl.ds(base + 8 * t, 8), :]
                value = jnp.where(inside, pltpu.roll(value, turn, 1), 0.0)
                partner[x, pl.ds(8 * t, 8), :] = value
                parts.append(value * lead[x, pl.ds(8 * t, 8), :])
        spectral = along_z(jnp.concatenate(parts, 0), weights)
        for q in range(BLOCK):
            row = stencil_row(block * BLOCK + q)
            one[pl.ds(row, BOX_Y), :] = spectral[q * BOX_Y : (q + 1) * BOX_Y]
        return 0

    lax.fori_loop(0, BOX_X // BLOCK, density_block, 0)

    sweep(one, three, centre + 6.0)
    sweep(three, one, centre)
    sweep(one, two, centre, three, 36.0)
    sweep(two, one, centre)
    sweep(one, three, centre, three, 1296.0)
    sweep(three, one, centre)
    sweep(one, two, centre)
    sweep(two, one, centre)
    sweep(one, two, centre)
    sweep(two, one, centre)
    sweep(one, two, centre, three, 46656.0)
    scale = 1.0 / (6.0 * 6.0 * 1296.0 * 46656.0)

    def potential_block(block, _):
        rows = jnp.concatenate(
            [two[pl.ds(stencil_row(block * BLOCK + q), BOX_Y), :] for q in range(BLOCK)], 0
        )
        potential = along_z(rows, weights) * scale
        for q in range(BLOCK):
            x = block * BLOCK + q
            for t in range(TILES):
                at = pl.ds(8 * t, 8)
                value = potential[q * BOX_Y + 8 * t : q * BOX_Y + 8 * t + 8]
                accum[lead_slot, x, at, :] = (
                    accum[lead_slot, x, at, :] + value * partner[x, at, :]
                )
                shift[pl.ds(shift_row(x) + 8 * t, 8), :] = value * lead[x, at, :]
        return 0

    lax.fori_loop(0, BOX_X // BLOCK, potential_block, 0)

    back_inside = (lane >= -gap_z) & (lane < BOX_Z - gap_z)
    back_turn = jnp.where(gap_z > 0, BOX_Z - gap_z, -gap_z)

    def back_block(block, _):
        for q in range(BLOCK):
            x = block * BLOCK + q
            base = (x + gap_x + MARGIN) * WIDE + MARGIN + gap_y
            for t in range(TILES):
                at = pl.ds(8 * t, 8)
                value = shift[pl.ds(base + 8 * t, 8), :]
                value = jnp.where(back_inside, pltpu.roll(value, back_turn, 1), 0.0)
                accum[partner_slot, x, at, :] = accum[partner_slot, x, at, :] + value
        return 0

    lax.fori_loop(0, BOX_X // BLOCK, back_block, 0)


REMOTE = 4
QUOTA = 2


def first_kernel(row, count, own, payload, note, sem):
    lane = lax.broadcasted_iota(jnp.int32, (8, BOX_Z), 1)
    value = jnp.where(lane == 2 * SLOTS, count[0].astype(F32), 0.0)
    for e in range(SLOTS):
        for k in range(2):
            value = jnp.where(lane == 2 * e + k, row[0, e, k].astype(F32), value)
    note[...] = jnp.zeros_like(note)
    note[0:8, :] = value
    box = pltpu.make_async_copy(own.at[0], payload.at[pl.ds(0, BOX_X)], sem.at[0])
    extra = pltpu.make_async_copy(note, payload.at[BOX_X], sem.at[1])
    box.start()
    extra.start()
    box.wait()
    extra.wait()


def second_kernel(own, box, sem):
    copy = pltpu.make_async_copy(own.at[1], box, sem)
    copy.start()
    copy.wait()


def stage_kernel(stage, row, count, position, offsets, weights, values, own, mate, *rest):
    if stage == 0:
        (accum, *rest) = rest
    elif stage == 1:
        (payload, _, accum, leaving, *rest) = rest
        remote = payload.at[pl.ds(0, BOX_X)]
    elif stage == 2:
        (payload, remote, _, accum, leaving, *rest) = rest
    else:
        (payload, _, accum, leaving, *rest) = rest
    lead, shift, partner, one, two, three, work, note, sem, note_sem = rest
    here = position[0]
    mate_id = here ^ 1
    is_left = here % 2 == 1
    across = jnp.where(is_left, here + 1, here - 1)

    if stage:
        copy = pltpu.make_async_copy(payload.at[BOX_X, pl.ds(0, 8), :], note, note_sem)
        copy.start()
        copy.wait()

    def near(e, k):
        return row[0, e, k]

    def far(e, k):
        return note[0, 2 * e + k].astype(jnp.int32)

    def place(orbital):
        device = orbital // ORB_DEV
        local_slot = orbital % ORB_DEV
        return jnp.where(
            device == here, local_slot, jnp.where(device == mate_id, 2 + local_slot, REMOTE)
        )

    work[0] = 0

    def push(wanted, lead_id, partner_id):
        @pl.when(wanted)
        def _():
            k = work[0]
            base = 1 + 5 * k
            work[0] = k + 1
            work[base] = place(lead_id)
            work[base + 1] = place(partner_id)
            for axis in range(3):
                work[base + 2 + axis] = offsets[3 * partner_id + axis] - offsets[3 * lead_id + axis]

    if stage in (0, 3):
        seen = jnp.int32(0)
        for e in range(SLOTS):
            lead_id, partner_id = near(e, 0), near(e, 1)
            inside = (
                (e < count[0])
                & (lead_id // ORB_DEV != across)
                & (partner_id // ORB_DEV != across)
            )
            early = seen < QUOTA
            push(inside & (early if stage == 0 else ~early), lead_id, partner_id)
            seen = seen + inside.astype(jnp.int32)
    if stage == 3:
        far_count = note[0, 2 * SLOTS].astype(jnp.int32)
        for e in range(SLOTS):
            lead_id, partner_id = far(e, 0), far(e, 1)
            push(
                (e < far_count)
                & (lead_id // ORB_DEV == here)
                & (partner_id // ORB_DEV == here),
                lead_id,
                partner_id,
            )
    if stage in (1, 2):
        far_count = note[0, 2 * SLOTS].astype(jnp.int32)
        left = jnp.where(is_left, here, across)
        right = jnp.where(is_left, across, here)
        entries = []
        load_left, load_right = jnp.int32(0), jnp.int32(0)
        for side in range(2):
            use_near = is_left if side == 0 else ~is_left
            other = right if side == 0 else left
            limit = jnp.where(use_near, count[0], far_count)
            for e in range(SLOTS):
                a = jnp.where(use_near, near(e, 0), far(e, 0))
                b = jnp.where(use_near, near(e, 1), far(e, 1))
                a_dev, b_dev = a // ORB_DEV, b // ORB_DEV
                on_left = (a_dev == left) | (b_dev == left)
                on_right = (a_dev == right) | (b_dev == right)
                crosses = (e < limit) & (
                    (a_dev == other) != (b_dev == other)
                )
                free = crosses & on_left & on_right
                fixed = crosses & ~free
                left_bit = jnp.where(a_dev == left, a, b) % ORB_DEV
                right_bit = jnp.where(a_dev == right, a, b) % ORB_DEV
                if side == 0:
                    load_left = load_left + fixed.astype(jnp.int32)
                else:
                    load_right = load_right + fixed.astype(jnp.int32)
                entries.append((side, a, b, free, fixed, left_bit, right_bit))
        for side, a, b, free, fixed, left_bit, right_bit in entries:
            go_left = (load_left < load_right) | (
                (load_left == load_right) & (right_bit <= left_bit)
            )
            load_left = load_left + (free & go_left).astype(jnp.int32)
            load_right = load_right + (free & ~go_left).astype(jnp.int32)
            at_left = (free & go_left) | (fixed if side == 0 else jnp.bool_(False))
            at_right = (free & ~go_left) | (fixed if side == 1 else jnp.bool_(False))
            mine = (at_left & is_left) | (at_right & ~is_left)
            bit = jnp.where(is_left, right_bit, left_bit)
            push(mine & (bit == stage - 1), a, b)

    total = work[0]
    sources = [own.at[0], own.at[1], mate.at[0], mate.at[1]]
    if stage in (1, 2):
        sources.append(remote)

    def window(buf):
        return shift.at[buf].reshape(SHIFT_PLANES, WIDE, BOX_Z).at[
            pl.ds(MARGIN, BOX_X), pl.ds(MARGIN, BOX_Y), :
        ]

    def fetch(k, buf):
        for which, target in ((0, lead.at[buf]), (1, window(buf))):
            slot = work[1 + 5 * k + which]
            for s, source in enumerate(sources):
                @pl.when(slot == s)
                def _():
                    pltpu.make_async_copy(source, target, sem.at[which, buf]).start()

    @pl.when(total > 0)
    def _():
        fetch(0, 0)
        for buf in (one, two, three):
            zero_borders(buf)
        zero_margins(shift.at[0])

        @pl.when(total > 1)
        def _():
            zero_margins(shift.at[1])

    if stage == 0:
        for slot in range(REMOTE + 1):
            zero_box(accum.at[slot])

    def visit(k, _):
        buf = k % 2
        pltpu.make_async_copy(sources[0], lead.at[buf], sem.at[0, buf]).wait()
        pltpu.make_async_copy(sources[0], window(buf), sem.at[1, buf]).wait()

        @pl.when(k + 1 < total)
        def _():
            fetch(k + 1, 1 - buf)

        base = 1 + 5 * k
        solve_pair(
            lead.at[buf], shift.at[buf], partner, (one, two, three), weights, values,
            [work[base + 2 + axis] for axis in range(3)], accum, work[base], work[base + 1],
        )
        return 0

    lax.fori_loop(0, total, visit, 0)

    if stage:
        boxes = accum.at[pl.ds(2, 2)] if stage == 3 else accum.at[REMOTE]
        copy = pltpu.make_async_copy(boxes, leaving, note_sem)
        copy.start()
        copy.wait()
    if stage == 1:
        @pl.when(total > 0)
        def _():
            zero_box(accum.at[REMOTE])


SMEM = pl.BlockSpec(memory_space=pltpu.SMEM)
VMEM = pl.BlockSpec(memory_space=pltpu.VMEM)
HBM = pl.BlockSpec(memory_space=pltpu.HBM)


def run_stage(stage, fixed, remote, accum):
    carried = [] if accum is None else [accum]
    operands = list(fixed) + list(remote) + carried
    specs = [SMEM] * 4 + [VMEM] * 2 + [HBM] * 2 + [HBM] * len(remote) + [VMEM] * len(carried)
    shapes = [jax.ShapeDtypeStruct((REMOTE + 1,) + BOX, F32)]
    outs = [VMEM]
    if stage:
        shapes.append(jax.ShapeDtypeStruct(((2,) if stage == 3 else ()) + BOX, F32))
        outs.append(VMEM)
    return pl.pallas_call(
        functools.partial(stage_kernel, stage),
        out_shape=shapes,
        in_specs=specs,
        out_specs=outs,
        input_output_aliases={len(operands) - 1: 0} if carried else {},
        scratch_shapes=[
            pltpu.VMEM((2,) + BOX, F32),
            pltpu.VMEM((2, SHIFT_ROWS, BOX_Z), F32),
            pltpu.VMEM(BOX, F32),
            pltpu.VMEM((STENCIL_ROWS, BOX_Z), F32),
            pltpu.VMEM((STENCIL_ROWS, BOX_Z), F32),
            pltpu.VMEM((STENCIL_ROWS, BOX_Z), F32),
            pltpu.SMEM((1 + 5 * 2 * SLOTS,), jnp.int32),
            pltpu.SMEM((8, BOX_Z), F32),
            pltpu.SemaphoreType.DMA((2, 2)),
            pltpu.SemaphoreType.DMA,
        ],
        compiler_params=pltpu.CompilerParams(vmem_limit_bytes=28 << 20),
        cost_estimate=pl.CostEstimate(
            flops=200_000_000, bytes_accessed=20_000_000, transcendentals=0
        ),
        name="stage_" + "abcd"[stage],
    )(*operands)


def total_kernel(box, accum, mate, remote, *rest):
    result, chunk, sem = rest[-3:]

    def add(x, _):
        for t in range(TILES):
            at = pl.ds(8 * t, 8)
            chunk[x, at, :] = accum[box, x, at, :] + mate[box, x, at, :] + remote[x, at, :]
        pltpu.make_async_copy(chunk.at[x], result.at[box, x], sem).start()
        return 0

    lax.fori_loop(0, BOX_X, add, 0, unroll=2)
    pltpu.make_async_copy(chunk, result.at[box], sem).wait()


def run_total(box, accum, mate, remote, result=None):
    operands = [accum, mate, remote]
    specs = [VMEM, VMEM, VMEM]
    aliases = {}
    if result is not None:
        operands.append(result)
        specs.append(HBM)
        aliases = {3: 0}
    return pl.pallas_call(
        functools.partial(total_kernel, box),
        out_shape=jax.ShapeDtypeStruct((ORB_DEV,) + BOX, F32),
        in_specs=specs,
        out_specs=HBM,
        input_output_aliases=aliases,
        scratch_shapes=[pltpu.VMEM(BOX, F32), pltpu.SemaphoreType.DMA],
        compiler_params=pltpu.CompilerParams(vmem_limit_bytes=4 << 20),
        name="total_" + "ab"[box],
    )(*operands)


def local(orbitals, pair_list, pair_count, box_offset):
    position = lax.axis_index("orb").astype(jnp.int32)[None]
    devices = lax.axis_size("orb")
    mates = [(d, d ^ 1) for d in range(devices)]
    across = [(d, d + 1) for d in range(1, devices - 1, 2)]
    across = across + [(b, a) for a, b in across]
    payload = pl.pallas_call(
        first_kernel,
        out_shape=jax.ShapeDtypeStruct((BOX_X + 1, BOX_Y, BOX_Z), F32),
        in_specs=[SMEM, SMEM, HBM],
        out_specs=HBM,
        scratch_shapes=[pltpu.VMEM((BOX_Y, BOX_Z), F32), pltpu.SemaphoreType.DMA((2,))],
        name="first_box",
    )(pair_list, pair_count, orbitals)
    payload, held = lax.optimization_barrier((payload, orbitals))
    far_first = lax.ppermute(payload, "orb", across)
    mate = lax.ppermute(held, "orb", mates)
    second = pl.pallas_call(
        second_kernel,
        out_shape=jax.ShapeDtypeStruct(BOX, F32),
        in_specs=[HBM],
        out_specs=HBM,
        scratch_shapes=[pltpu.SemaphoreType.DMA],
        name="second_box",
    )(held)
    far_second = lax.ppermute(second, "orb", across)
    weights, values = sine_basis()
    fixed = (
        pair_list, pair_count, position, box_offset.reshape(-1),
        jnp.asarray(weights), jnp.asarray(values), orbitals, mate,
    )
    (accum,) = run_stage(0, fixed, (), None)
    accum, for_first = run_stage(1, fixed, (far_first,), accum)
    back_first = lax.ppermute(for_first, "orb", across)
    accum, for_second = run_stage(2, fixed, (far_first, far_second), accum)
    for_second, back_first, accum = lax.optimization_barrier((for_second, back_first, accum))
    back_second = lax.ppermute(for_second, "orb", across)
    accum, for_mate = run_stage(3, fixed, (far_first,), accum)
    back_mate = lax.ppermute(for_mate, "orb", mates)
    result = run_total(0, accum, back_mate, back_first)
    return run_total(1, accum, back_mate, back_second, result)


def solution(mesh):
    placed = (P("orb", None, None, None), P("orb", None, None), P("orb"), P())
    return jax.shard_map(
        local, mesh=mesh, in_specs=placed, out_specs=P("orb", None, None, None), check_vma=False
    )
```

profile of v0, /device:TPU:80, one launch (start us, length us, event | category | flops | bytes accessed | tf_op | source)
XLA Modules:
  0.0 204.6 jit_solution(7987102349114638216)
XLA Ops:
  0.7 1.4 copy.21.row
  2.0 49.5 %first_box.1 = f32[49,64,128]{2,1,0:T(8,128)} custom-call(s32[1,6,2]{2,1,0:T(8,128)} %copy.21.row, s32[1]{0:T(128)S(6)} %copy.26.count, f32[2,48,64,128]{3,2,1,0:T(8,128)} %own.10), custom_call_target="tpu_custom_call" | custom-call | tf_op jit(solution)/shard_map/first_box/pallas_call | solution.py:469
  51.5 0.0 copy-start.3
  51.5 0.0 copy-start
  51.5 0.0 copy-start.2
  51.6 0.1 collective-permute-start
  51.7 4.3 %collective-permute-start.1 = (f32[49,64,128]{2,1,0:T(8,128)}, f32[49,64,128]{2,1,0:T(8,128)}, u32[]{:S(2)}, u32[]{:S(2)}) collective-permute-start(f32[49,64,128]{2,1,0:T(8,128)} %first_box.1), channel_id=1, source_target_pairs={{1,2},{3,4},{5,6},{7,8},{9,10},{11,12},{13,14},{15,16},{17,18},{19... | collective-permute-start | bytes 4816904 | tf_op jit(solution)/shard_map/ppermute | solution.py:478
  56.0 48.8 %second_box.1 = f32[48,64,128]{2,1,0:T(8,128)} custom-call(f32[2,48,64,128]{3,2,1,0:T(8,128)} %own.10), custom_call_target="tpu_custom_call" | custom-call | tf_op jit(solution)/shard_map/second_box/pallas_call | solution.py:480
  104.7 3.4 %collective-permute-start.2 = (f32[48,64,128]{2,1,0:T(8,128)}, f32[48,64,128]{2,1,0:T(8,128)}, u32[]{:S(2)}, u32[]{:S(2)}) collective-permute-start(f32[48,64,128]{2,1,0:T(8,128)} %second_box.1), channel_id=1, source_target_pairs={{1,2},{3,4},{5,6},{7,8},{9,10},{11,12},{13,14},{15,16},{17,18},{19... | collective-permute-start | bytes 4718600 | tf_op jit(solution)/shard_map/ppermute | solution.py:488
  108.1 0.1 copy.16
  108.3 0.2 reshape.3.offsets
  108.5 0.0 collective-permute-done.mate
  108.5 17.9 %stage_a.1.rest_1_ = f32[5,48,64,128]{3,2,1,0:T(8,128)S(1)} custom-call(s32[1,6,2]{2,1,0:T(8,128)S(1)} %copy-done.1, s32[1]{0:T(128)S(6)} %copy.26.count, s32[1]{0:T(128)} %bitcast.position, s32[768]{0:T(1024)S(1)} %reshape.3.offsets, bf16[256,256]{1,0:T(8,128)(2,1)S(1)} %copy-done, f32[8,128]{1,0:T(8,128)S(1)} %copy-done.2, f32[2,48,64,128]{3,2,1,0:T(8,128)} %own.10, ...), custom_call_target="tpu_custom_call" | custom-call | flops 200000000 | bytes 20000000 | tf_op jit(solution)/shard_map/stage_a/pallas_call | solution.py:403
  126.4 11.0 %stage_b.1 = (f32[5,48,64,128]{3,2,1,0:T(8,128)S(1)}, f32[48,64,128]{2,1,0:T(8,128)S(1)}) custom-call(s32[1,6,2]{2,1,0:T(8,128)S(1)} %copy-done.1, s32[1]{0:T(128)S(6)} %copy.26.count, s32[1]{0:T(128)} %bitcast.position, s32[768]{0:T(1024)S(1)} %reshape.3.offsets, bf16[256,256]{1,0:T(8,128)(2,1)S(1)} %copy-done, ...), custom_call_target="tpu_custom_call", output_to_operand_aliasing={{0}: (9, {})} | custom-call | flops 200000000 | bytes 20000000 | tf_op jit(solution)/shard_map/stage_b/pallas_call | solution.py:403
  137.5 4.1 %collective-permute-start.3 = (f32[48,64,128]{2,1,0:T(8,128)S(1)}, f32[48,64,128]{2,1,0:T(8,128)S(1)}, u32[]{:S(2)}, u32[]{:S(2)}) collective-permute-start(f32[48,64,128]{2,1,0:T(8,128)S(1)} %get-tuple-element.20), channel_id=1, source_target_pairs={{1,2},{3,4},{5,6},{7,8},{9,10},{11,12},{13,14},{15,16},{17,18},{19... | collective-permute-start | bytes 4718600 | tf_op jit(solution)/shard_map/ppermute | solution.py:496
  141.6 10.8 %stage_c.1 = (f32[5,48,64,128]{3,2,1,0:T(8,128)S(1)}, f32[48,64,128]{2,1,0:T(8,128)S(1)}) custom-call(s32[1,6,2]{2,1,0:T(8,128)S(1)} %copy-done.1, s32[1]{0:T(128)S(6)} %copy.26.count, s32[1]{0:T(128)} %bitcast.position, s32[768]{0:T(1024)S(1)} %reshape.3.offsets, bf16[256,256]{1,0:T(8,128)(2,1)S(1)} %copy-done, ...), custom_call_target="tpu_custom_call", output_to_operand_aliasing={{0}: (10, {})} | custom-call | flops 200000000 | bytes 20000000 | tf_op jit(solution)/shard_map/stage_c/pallas_call | solution.py:403
  152.5 8.8 %collective-permute-done.3.remote = f32[48,64,128]{2,1,0:T(8,128)S(1)} collective-permute-done((f32[48,64,128]{2,1,0:T(8,128)S(1)}, f32[48,64,128]{2,1,0:T(8,128)S(1)}, u32[]{:S(2)}, u32[]{:S(2)}) %collective-permute-start.3) | collective-permute-done | bytes 1572896 | tf_op jit(solution)/shard_map/ppermute | solution.py:496
  161.3 18.2 %stage_d.1 = (f32[5,48,64,128]{3,2,1,0:T(8,128)S(1)}, f32[2,48,64,128]{3,2,1,0:T(8,128)S(1)}) custom-call(s32[1,6,2]{2,1,0:T(8,128)S(1)} %copy-done.1, s32[1]{0:T(128)S(6)} %copy.26.count, s32[1]{0:T(128)} %bitcast.position, s32[768]{0:T(1024)S(1)} %reshape.3.offsets, bf16[256,256]{1,0:T(8,128)(2,1)S(1)} %copy-done, ...), custom_call_target="tpu_custom_call", output_to_operand_aliasing={{0}: (9, {})} | custom-call | flops 200000000 | bytes 20000000 | tf_op jit(solution)/shard_map/stage_d/pallas_call | solution.py:403
  179.5 0.1 collective-permute-start.4
  179.6 1.9 collective-permute-start.5
  181.5 3.7 %collective-permute-done.4.mate = f32[2,48,64,128]{3,2,1,0:T(8,128)S(1)} collective-permute-done((f32[2,48,64,128]{3,2,1,0:T(8,128)S(1)}, f32[2,48,64,128]{3,2,1,0:T(8,128)S(1)}, u32[]{:S(2)}, u32[]{:S(2)}) %collective-permute-start.4) | collective-permute-done | bytes 3145760 | tf_op jit(solution)/shard_map/ppermute | solution.py:501
  185.2 1.1 total_a.1.rest_0_
  186.4 17.1 %collective-permute-done.5.remote = f32[48,64,128]{2,1,0:T(8,128)S(1)} collective-permute-done((f32[48,64,128]{2,1,0:T(8,128)S(1)}, f32[48,64,128]{2,1,0:T(8,128)S(1)}, u32[]{:S(2)}, u32[]{:S(2)}) %collective-permute-start.5) | collective-permute-done | bytes 1572896 | tf_op jit(solution)/shard_map/ppermute | solution.py:499
  203.4 1.1 total_b.1
  (7 shorter events, 0.0 us)
Async XLA Ops:
  51.5 56.6 %copy-start.3 = (s32[256,3]{0,1:T(4,128)S(1)}, s32[256,3]{0,1:T(4,128)}, u32[]{:S(2)}) copy-start(s32[256,3]{0,1:T(4,128)} %param.9) | copy-start | bytes 9220
  51.5 57.0 %copy-start = (bf16[256,256]{1,0:T(8,128)(2,1)S(1)}, bf16[256,256]{1,0:T(8,128)(2,1)}, u32[]{:S(2)}) copy-start(bf16[256,256]{1,0:T(8,128)(2,1)} %constant.8.clone.weights) | copy-start | bytes 393220
  51.5 57.0 %copy-start.1 = (s32[1,6,2]{2,1,0:T(8,128)S(1)}, s32[1,6,2]{2,1,0:T(8,128)}, u32[]{:S(2)}) copy-start(s32[1,6,2]{2,1,0:T(8,128)} %copy.21.row) | copy-start | bytes 148
  51.5 57.0 %copy-start.2 = (f32[8,128]{1,0:T(8,128)S(1)}, f32[8,128]{1,0:T(8,128)}, u32[]{:S(2)}) copy-start(f32[8,128]{1,0:T(8,128)} %constant.9.clone.values) | copy-start | bytes 12292
  51.6 56.9 %collective-permute-start = (f32[2,48,64,128]{3,2,1,0:T(8,128)}, f32[2,48,64,128]{3,2,1,0:T(8,128)S(1)}, u32[]{:S(2)}, u32[]{:S(2)}) collective-permute-start(f32[2,48,64,128]{3,2,1,0:T(8,128)} %own.10), channel_id=1, source_target_pairs={{0,1},{1,0},{2,3},{3,2},{4,5},{5,4},{6,7},{7,6},{8,9},{9,8},{10,11... | collective-permute-start | bytes 9437192 | tf_op jit(solution)/shard_map/ppermute | solution.py:479
  51.7 74.8 %collective-permute-start.1 = (f32[49,64,128]{2,1,0:T(8,128)}, f32[49,64,128]{2,1,0:T(8,128)}, u32[]{:S(2)}, u32[]{:S(2)}) collective-permute-start(f32[49,64,128]{2,1,0:T(8,128)} %first_box.1), channel_id=1, source_target_pairs={{1,2},{3,4},{5,6},{7,8},{9,10},{11,12},{13,14},{15,16},{17,18},{19... | collective-permute-start | bytes 4816904 | tf_op jit(solution)/shard_map/ppermute | solution.py:478
  104.7 36.9 %collective-permute-start.2 = (f32[48,64,128]{2,1,0:T(8,128)}, f32[48,64,128]{2,1,0:T(8,128)}, u32[]{:S(2)}, u32[]{:S(2)}) collective-permute-start(f32[48,64,128]{2,1,0:T(8,128)} %second_box.1), channel_id=1, source_target_pairs={{1,2},{3,4},{5,6},{7,8},{9,10},{11,12},{13,14},{15,16},{17,18},{19... | collective-permute-start | bytes 4718600 | tf_op jit(solution)/shard_map/ppermute | solution.py:488
  137.5 23.8 %collective-permute-start.3 = (f32[48,64,128]{2,1,0:T(8,128)S(1)}, f32[48,64,128]{2,1,0:T(8,128)S(1)}, u32[]{:S(2)}, u32[]{:S(2)}) collective-permute-start(f32[48,64,128]{2,1,0:T(8,128)S(1)} %get-tuple-element.20), channel_id=1, source_target_pairs={{1,2},{3,4},{5,6},{7,8},{9,10},{11,12},{13,14},{15,16},{17,18},{19... | collective-permute-start | bytes 4718600 | tf_op jit(solution)/shard_map/ppermute | solution.py:496
  179.5 5.7 %collective-permute-start.4 = (f32[2,48,64,128]{3,2,1,0:T(8,128)S(1)}, f32[2,48,64,128]{3,2,1,0:T(8,128)S(1)}, u32[]{:S(2)}, u32[]{:S(2)}) collective-permute-start(f32[2,48,64,128]{3,2,1,0:T(8,128)S(1)} %get-tuple-element.24), channel_id=1, source_target_pairs={{0,1},{1,0},{2,3},{3,2},{4,5},{5,4},{6,7},{7,6},{8,9},{9,8},{10,11... | collective-permute-start | bytes 9437192 | tf_op jit(solution)/shard_map/ppermute | solution.py:501
  179.6 23.8 %collective-permute-start.5 = (f32[48,64,128]{2,1,0:T(8,128)S(1)}, f32[48,64,128]{2,1,0:T(8,128)S(1)}, u32[]{:S(2)}, u32[]{:S(2)}) collective-permute-start(f32[48,64,128]{2,1,0:T(8,128)S(1)} %get-tuple-element.25), channel_id=1, source_target_pairs={{1,2},{3,4},{5,6},{7,8},{9,10},{11,12},{13,14},{15,16},{17,18},{19... | collective-permute-start | bytes 4718600 | tf_op jit(solution)/shard_map/ppermute | solution.py:499
where the time goes:
time: 208 us; the launch traced here: 205 us
  Pallas kernels  158 us (76%)
  waiting for transfers between devices  29.6 us (14%)
  starting transfers between devices  13.9 us (7%)
    pallas_call x4, Pallas kernels, run_stage(): pl.pallas_call(functools.partial(stage_kernel, stage), out_shape=shapes,...  58 us
    pallas_call x1, Pallas kernels, local(): pl.pallas_call(first_kernel, out_shape=jax.ShapeDtypeStruct((BOX_X + 1, B...  49.5 us
    pallas_call x1, Pallas kernels, local(): pl.pallas_call(second_kernel, out_shape=jax.ShapeDtypeStruct(BOX, F32), i...  48.8 us
    ppermute x1, waiting for transfers between devices, local(): back_second = lax.ppermute(for_second, 'orb', across)  17.1 us
    ppermute x1, waiting for transfers between devices, local(): back_first = lax.ppermute(for_first, 'orb', across)  8.84 us
    ppermute x1, starting transfers between devices, local(): far_first = lax.ppermute(payload, 'orb', across)  4.3 us
  transfers between devices with their start and end apart: 6, of which 3 were waited for; matrix products, arithmetic and copies ran while one was open for 0% of the time, Pallas kernels for 44%

commit v1 on v0

--- a/solution.py
+++ b/solution.py
@@ -21,7 +21,7 @@
 SHIFT_PLANES = BOX_X + 2 * MARGIN + 1
 SHIFT_ROWS = SHIFT_PLANES * WIDE
 STENCIL_UNROLL = 8
-BLOCK = 16
+BLOCK = 24
 F32 = jnp.float32
 BF16 = jnp.bfloat16
 
@@ -192,20 +192,17 @@
 QUOTA = 2
 
 
-def first_kernel(row, count, own, payload, note, sem):
+def first_kernel(row, count, own, payload, sem):
+    box = pltpu.make_async_copy(own.at[0], payload.at[pl.ds(0, BOX_X)], sem)
+    box.start()
     lane = lax.broadcasted_iota(jnp.int32, (8, BOX_Z), 1)
     value = jnp.where(lane == 2 * SLOTS, count[0].astype(F32), 0.0)
     for e in range(SLOTS):
         for k in range(2):
             value = jnp.where(lane == 2 * e + k, row[0, e, k].astype(F32), value)
-    note[...] = jnp.zeros_like(note)
-    note[0:8, :] = value
-    box = pltpu.make_async_copy(own.at[0], payload.at[pl.ds(0, BOX_X)], sem.at[0])
-    extra = pltpu.make_async_copy(note, payload.at[BOX_X], sem.at[1])
-    box.start()
-    extra.start()
+    payload[BOX_X] = jnp.zeros((BOX_Y, BOX_Z), F32)
+    payload[BOX_X, 0:8, :] = value
     box.wait()
-    extra.wait()
 
 
 def second_kernel(own, box, sem):
@@ -470,8 +467,8 @@
         first_kernel,
         out_shape=jax.ShapeDtypeStruct((BOX_X + 1, BOX_Y, BOX_Z), F32),
         in_specs=[SMEM, SMEM, HBM],
-        out_specs=HBM,
-        scratch_shapes=[pltpu.VMEM((BOX_Y, BOX_Z), F32), pltpu.SemaphoreType.DMA((2,))],
+        out_specs=VMEM,
+        scratch_shapes=[pltpu.SemaphoreType.DMA],
         name="first_box",
     )(pair_list, pair_count, orbitals)
     payload, held = lax.optimization_barrier((payload, orbitals))
@@ -481,7 +478,7 @@
         second_kernel,
         out_shape=jax.ShapeDtypeStruct(BOX, F32),
         in_specs=[HBM],
-        out_specs=HBM,
+        out_specs=VMEM,
         scratch_shapes=[pltpu.SemaphoreType.DMA],
         name="second_box",
     )(held)

time: 208 us -> 119 us (0.57)
  the two profiles are of different devices: /device:TPU:80 before, /device:TPU:79 now
where the time goes in v1:
time: 119 us
  starting transfers between devices  43.6 us (37%)
  waiting for transfers between devices  41.2 us (35%)
  Pallas kernels  31.5 us (26%)
  local copies, waits for them, and re-layouts  1.72 us (1%)
    ppermute x1, starting transfers between devices, local(): back_mate = lax.ppermute(for_mate, 'orb', mates)  26.8 us
    pallas_call x4, Pallas kernels, run_stage(): pl.pallas_call(functools.partial(stage_kernel, stage), out_shape=shapes,...  23.4 us
    ppermute x1, waiting for transfers between devices, local(): back_second = lax.ppermute(for_second, 'orb', across)  17.4 us
    ppermute x1, waiting for transfers between devices, local(): far_first = lax.ppermute(payload, 'orb', across)  12.3 us
    ppermute x1, waiting for transfers between devices, local(): far_second = lax.ppermute(second, 'orb', across)  8.12 us
    ppermute x1, starting transfers between devices, local(): back_first = lax.ppermute(for_first, 'orb', across)  6.49 us
    ppermute x1, starting transfers between devices, local(): far_second = lax.ppermute(second, 'orb', across)  4.59 us
    ppermute x1, waiting for transfers between devices, local(): back_mate = lax.ppermute(for_mate, 'orb', mates)  3.37 us
  transfers between devices with their start and end apart: 6, of which 4 were waited for; matrix products, arithmetic and copies ran while one was open for 0% of the time, Pallas kernels for 21%

profile of v1, /device:TPU:79, one launch (start us, length us, event | category | flops | bytes accessed | tf_op | source)
XLA Modules:
  0.0 118.8 jit_solution(12886275132341970430)
XLA Ops:
  0.7 1.4 %copy.21.row = s32[1,6,2]{2,1,0:T(8,128)} copy(s32[1,6,2]{1,2,0:T(2,128)} %param.7) | data formatting | bytes 96 | tf_op args[1]
  2.0 3.3 %first_box.1 = f32[49,64,128]{2,1,0:T(8,128)} custom-call(s32[1,6,2]{2,1,0:T(8,128)} %copy.21.row, s32[1]{0:T(128)S(6)} %copy.26.count, f32[2,48,64,128]{3,2,1,0:T(8,128)} %own.10), custom_call_target="tpu_custom_call" | custom-call | tf_op jit(solution)/shard_map/first_box/pallas_call | solution.py:466
  5.3 0.0 copy-start.3
  5.3 0.0 copy-start
  5.3 0.0 copy-start.2
  5.3 0.8 collective-permute-start
  6.1 3.1 %collective-permute-start.1 = (f32[49,64,128]{2,1,0:T(8,128)}, f32[49,64,128]{2,1,0:T(8,128)}, u32[]{:S(2)}, u32[]{:S(2)}) collective-permute-start(f32[49,64,128]{2,1,0:T(8,128)} %first_box.1), channel_id=1, source_target_pairs={{1,2},{3,4},{5,6},{7,8},{9,10},{11,12},{13,14},{15,16},{17,18},{19... | collective-permute-start | bytes 4816904 | tf_op jit(solution)/shard_map/ppermute | solution.py:475
  9.2 2.6 %second_box.1 = f32[48,64,128]{2,1,0:T(8,128)} custom-call(f32[2,48,64,128]{3,2,1,0:T(8,128)} %own.10), custom_call_target="tpu_custom_call" | custom-call | tf_op jit(solution)/shard_map/second_box/pallas_call | solution.py:477
  11.7 4.6 %collective-permute-start.2 = (f32[48,64,128]{2,1,0:T(8,128)}, f32[48,64,128]{2,1,0:T(8,128)}, u32[]{:S(2)}, u32[]{:S(2)}) collective-permute-start(f32[48,64,128]{2,1,0:T(8,128)} %second_box.1), channel_id=1, source_target_pairs={{1,2},{3,4},{5,6},{7,8},{9,10},{11,12},{13,14},{15,16},{17,18},{19... | collective-permute-start | bytes 4718600 | tf_op jit(solution)/shard_map/ppermute | solution.py:485
  16.4 0.1 copy.16
  16.5 0.2 reshape.3.offsets
  16.8 1.6 %stage_a.1.rest_1_ = f32[5,48,64,128]{3,2,1,0:T(8,128)S(1)} custom-call(s32[1,6,2]{2,1,0:T(8,128)S(1)} %copy-done.1, s32[1]{0:T(128)S(6)} %copy.26.count, s32[1]{0:T(128)} %bitcast.position, s32[768]{0:T(1024)S(1)} %reshape.3.offsets, bf16[256,256]{1,0:T(8,128)(2,1)S(1)} %copy-done, f32[8,128]{1,0:T(8,128)S(1)} %copy-done.2, f32[2,48,64,128]{3,2,1,0:T(8,128)} %own.10, ...), custom_call_target="tpu_custom_call" | custom-call | flops 200000000 | bytes 20000000 | tf_op jit(solution)/shard_map/stage_a/pallas_call | solution.py:400
  18.3 12.3 %collective-permute-done.1.rest_0_ = f32[49,64,128]{2,1,0:T(8,128)} collective-permute-done((f32[49,64,128]{2,1,0:T(8,128)}, f32[49,64,128]{2,1,0:T(8,128)}, u32[]{:S(2)}, u32[]{:S(2)}) %collective-permute-start.1) | collective-permute-done | bytes 1605664 | tf_op jit(solution)/shard_map/ppermute | solution.py:475
  30.6 2.2 %stage_b.1 = (f32[5,48,64,128]{3,2,1,0:T(8,128)S(1)}, f32[48,64,128]{2,1,0:T(8,128)S(1)}) custom-call(s32[1,6,2]{2,1,0:T(8,128)S(1)} %copy-done.1, s32[1]{0:T(128)S(6)} %copy.26.count, s32[1]{0:T(128)} %bitcast.position, s32[768]{0:T(1024)S(1)} %reshape.3.offsets, bf16[256,256]{1,0:T(8,128)(2,1)S(1)} %copy-done, ...), custom_call_target="tpu_custom_call", output_to_operand_aliasing={{0}: (9, {})} | custom-call | flops 200000000 | bytes 20000000 | tf_op jit(solution)/shard_map/stage_b/pallas_call | solution.py:400
  32.8 6.5 %collective-permute-start.3 = (f32[48,64,128]{2,1,0:T(8,128)S(1)}, f32[48,64,128]{2,1,0:T(8,128)S(1)}, u32[]{:S(2)}, u32[]{:S(2)}) collective-permute-start(f32[48,64,128]{2,1,0:T(8,128)S(1)} %get-tuple-element.20), channel_id=1, source_target_pairs={{1,2},{3,4},{5,6},{7,8},{9,10},{11,12},{13,14},{15,16},{17,18},{19... | collective-permute-start | bytes 4718600 | tf_op jit(solution)/shard_map/ppermute | solution.py:493
  39.3 8.1 %collective-permute-done.2.rest_1_ = f32[48,64,128]{2,1,0:T(8,128)} collective-permute-done((f32[48,64,128]{2,1,0:T(8,128)}, f32[48,64,128]{2,1,0:T(8,128)}, u32[]{:S(2)}, u32[]{:S(2)}) %collective-permute-start.2) | collective-permute-done | bytes 1572896 | tf_op jit(solution)/shard_map/ppermute | solution.py:485
  47.5 17.6 %stage_c.1 = (f32[5,48,64,128]{3,2,1,0:T(8,128)S(1)}, f32[48,64,128]{2,1,0:T(8,128)S(1)}) custom-call(s32[1,6,2]{2,1,0:T(8,128)S(1)} %copy-done.1, s32[1]{0:T(128)S(6)} %copy.26.count, s32[1]{0:T(128)} %bitcast.position, s32[768]{0:T(1024)S(1)} %reshape.3.offsets, bf16[256,256]{1,0:T(8,128)(2,1)S(1)} %copy-done, ...), custom_call_target="tpu_custom_call", output_to_operand_aliasing={{0}: (10, {})} | custom-call | flops 200000000 | bytes 20000000 | tf_op jit(solution)/shard_map/stage_c/pallas_call | solution.py:400
  65.1 2.0 %stage_d.1 = (f32[5,48,64,128]{3,2,1,0:T(8,128)S(1)}, f32[2,48,64,128]{3,2,1,0:T(8,128)S(1)}) custom-call(s32[1,6,2]{2,1,0:T(8,128)S(1)} %copy-done.1, s32[1]{0:T(128)S(6)} %copy.26.count, s32[1]{0:T(128)} %bitcast.position, s32[768]{0:T(1024)S(1)} %reshape.3.offsets, bf16[256,256]{1,0:T(8,128)(2,1)S(1)} %copy-done, ...), custom_call_target="tpu_custom_call", output_to_operand_aliasing={{0}: (9, {})} | custom-call | flops 200000000 | bytes 20000000 | tf_op jit(solution)/shard_map/stage_d/pallas_call | solution.py:400
  67.1 26.8 %collective-permute-start.4 = (f32[2,48,64,128]{3,2,1,0:T(8,128)S(1)}, f32[2,48,64,128]{3,2,1,0:T(8,128)S(1)}, u32[]{:S(2)}, u32[]{:S(2)}) collective-permute-start(f32[2,48,64,128]{3,2,1,0:T(8,128)S(1)} %get-tuple-element.24), channel_id=1, source_target_pairs={{0,1},{1,0},{2,3},{3,2},{4,5},{5,4},{6,7},{7,6},{8,9},{9,8},{10,11... | collective-permute-start | bytes 9437192 | tf_op jit(solution)/shard_map/ppermute | solution.py:498
  93.9 1.9 %collective-permute-start.5 = (f32[48,64,128]{2,1,0:T(8,128)S(1)}, f32[48,64,128]{2,1,0:T(8,128)S(1)}, u32[]{:S(2)}, u32[]{:S(2)}) collective-permute-start(f32[48,64,128]{2,1,0:T(8,128)S(1)} %get-tuple-element.25), channel_id=1, source_target_pairs={{1,2},{3,4},{5,6},{7,8},{9,10},{11,12},{13,14},{15,16},{17,18},{19... | collective-permute-start | bytes 4718600 | tf_op jit(solution)/shard_map/ppermute | solution.py:496
  95.8 3.4 %collective-permute-done.4.mate = f32[2,48,64,128]{3,2,1,0:T(8,128)S(1)} collective-permute-done((f32[2,48,64,128]{3,2,1,0:T(8,128)S(1)}, f32[2,48,64,128]{3,2,1,0:T(8,128)S(1)}, u32[]{:S(2)}, u32[]{:S(2)}) %collective-permute-start.4) | collective-permute-done | bytes 3145760 | tf_op jit(solution)/shard_map/ppermute | solution.py:498
  99.2 1.1 total_a.1.rest_0_
  100.3 17.4 %collective-permute-done.5.remote = f32[48,64,128]{2,1,0:T(8,128)S(1)} collective-permute-done((f32[48,64,128]{2,1,0:T(8,128)S(1)}, f32[48,64,128]{2,1,0:T(8,128)S(1)}, u32[]{:S(2)}, u32[]{:S(2)}) %collective-permute-start.5) | collective-permute-done | bytes 1572896 | tf_op jit(solution)/shard_map/ppermute | solution.py:496
  117.7 1.1 total_b.1
  (7 shorter events, 0.0 us)
Async XLA Ops:
  5.3 11.1 %copy-start.3 = (s32[256,3]{0,1:T(4,128)S(1)}, s32[256,3]{0,1:T(4,128)}, u32[]{:S(2)}) copy-start(s32[256,3]{0,1:T(4,128)} %param.9) | copy-start | bytes 9220
  5.3 11.4 %copy-start = (bf16[256,256]{1,0:T(8,128)(2,1)S(1)}, bf16[256,256]{1,0:T(8,128)(2,1)}, u32[]{:S(2)}) copy-start(bf16[256,256]{1,0:T(8,128)(2,1)} %constant.8.clone.weights) | copy-start | bytes 393220
  5.3 11.4 %copy-start.1 = (s32[1,6,2]{2,1,0:T(8,128)S(1)}, s32[1,6,2]{2,1,0:T(8,128)}, u32[]{:S(2)}) copy-start(s32[1,6,2]{2,1,0:T(8,128)} %copy.21.row) | copy-start | bytes 148
  5.3 11.4 %copy-start.2 = (f32[8,128]{1,0:T(8,128)S(1)}, f32[8,128]{1,0:T(8,128)}, u32[]{:S(2)}) copy-start(f32[8,128]{1,0:T(8,128)} %constant.9.clone.values) | copy-start | bytes 12292
  5.3 11.4 %collective-permute-start = (f32[2,48,64,128]{3,2,1,0:T(8,128)}, f32[2,48,64,128]{3,2,1,0:T(8,128)S(1)}, u32[]{:S(2)}, u32[]{:S(2)}) collective-permute-start(f32[2,48,64,128]{3,2,1,0:T(8,128)} %own.10), channel_id=1, source_target_pairs={{0,1},{1,0},{2,3},{3,2},{4,5},{5,4},{6,7},{7,6},{8,9},{9,8},{10,11... | collective-permute-start | bytes 9437192 | tf_op jit(solution)/shard_map/ppermute | solution.py:476
  6.1 24.5 %collective-permute-start.1 = (f32[49,64,128]{2,1,0:T(8,128)}, f32[49,64,128]{2,1,0:T(8,128)}, u32[]{:S(2)}, u32[]{:S(2)}) collective-permute-start(f32[49,64,128]{2,1,0:T(8,128)} %first_box.1), channel_id=1, source_target_pairs={{1,2},{3,4},{5,6},{7,8},{9,10},{11,12},{13,14},{15,16},{17,18},{19... | collective-permute-start | bytes 4816904 | tf_op jit(solution)/shard_map/ppermute | solution.py:475
  11.7 35.7 %collective-permute-start.2 = (f32[48,64,128]{2,1,0:T(8,128)}, f32[48,64,128]{2,1,0:T(8,128)}, u32[]{:S(2)}, u32[]{:S(2)}) collective-permute-start(f32[48,64,128]{2,1,0:T(8,128)} %second_box.1), channel_id=1, source_target_pairs={{1,2},{3,4},{5,6},{7,8},{9,10},{11,12},{13,14},{15,16},{17,18},{19... | collective-permute-start | bytes 4718600 | tf_op jit(solution)/shard_map/ppermute | solution.py:485
  32.8 32.3 %collective-permute-start.3 = (f32[48,64,128]{2,1,0:T(8,128)S(1)}, f32[48,64,128]{2,1,0:T(8,128)S(1)}, u32[]{:S(2)}, u32[]{:S(2)}) collective-permute-start(f32[48,64,128]{2,1,0:T(8,128)S(1)} %get-tuple-element.20), channel_id=1, source_target_pairs={{1,2},{3,4},{5,6},{7,8},{9,10},{11,12},{13,14},{15,16},{17,18},{19... | collective-permute-start | bytes 4718600 | tf_op jit(solution)/shard_map/ppermute | solution.py:493
  67.1 32.1 %collective-permute-start.4 = (f32[2,48,64,128]{3,2,1,0:T(8,128)S(1)}, f32[2,48,64,128]{3,2,1,0:T(8,128)S(1)}, u32[]{:S(2)}, u32[]{:S(2)}) collective-permute-start(f32[2,48,64,128]{3,2,1,0:T(8,128)S(1)} %get-tuple-element.24), channel_id=1, source_target_pairs={{0,1},{1,0},{2,3},{3,2},{4,5},{5,4},{6,7},{7,6},{8,9},{9,8},{10,11... | collective-permute-start | bytes 9437192 | tf_op jit(solution)/shard_map/ppermute | solution.py:498
  93.9 23.8 %collective-permute-start.5 = (f32[48,64,128]{2,1,0:T(8,128)S(1)}, f32[48,64,128]{2,1,0:T(8,128)S(1)}, u32[]{:S(2)}, u32[]{:S(2)}) collective-permute-start(f32[48,64,128]{2,1,0:T(8,128)S(1)} %get-tuple-element.25), channel_id=1, source_target_pairs={{1,2},{3,4},{5,6},{7,8},{9,10},{11,12},{13,14},{15,16},{17,18},{19... | collective-permute-start | bytes 4718600 | tf_op jit(solution)/shard_map/ppermute | solution.py:496

commit v2 on v0

--- a/solution.py
+++ b/solution.py
@@ -18,10 +18,11 @@
 STENCIL_ROWS = (BOX_X + 2) * PLANE + 8
 MARGIN = 24
 WIDE = BOX_Y + MARGIN
-SHIFT_PLANES = BOX_X + 2 * MARGIN + 1
+SHIFT_PLANES = BOX_X + 2
 SHIFT_ROWS = SHIFT_PLANES * WIDE
 STENCIL_UNROLL = 8
-BLOCK = 16
+BLOCK = 24
+CHUNKS = 6
 F32 = jnp.float32
 BF16 = jnp.bfloat16
 
@@ -42,7 +43,11 @@
 
 
 def shift_row(x):
-    return pl.multiple_of((x + MARGIN) * WIDE + MARGIN, 8)
+    return pl.multiple_of((x + 1) * WIDE + MARGIN, 8)
+
+
+def shifted_plane(x):
+    return jnp.where((x >= 0) & (x < BOX_X), x + 1, 0) * WIDE + MARGIN
 
 
 def zero_rows(ref, first, rows):
@@ -51,17 +56,14 @@
 
 
 def zero_margins(ref):
+    zero_rows(ref, 0, WIDE)
+    zero_rows(ref, SHIFT_ROWS - WIDE, WIDE)
+
     def plane(p, _):
-        row = pl.multiple_of(p * WIDE, 8)
-        zero_rows(ref, row, MARGIN)
-
-        @pl.when((p < MARGIN) | (p >= MARGIN + BOX_X))
-        def _():
-            zero_rows(ref, row + MARGIN, BOX_Y)
-
-        return 0
-
-    lax.fori_loop(0, SHIFT_PLANES, plane, 0)
+        zero_rows(ref, pl.multiple_of((p + 1) * WIDE, 8), MARGIN)
+        return 0
+
+    lax.fori_loop(0, BOX_X, plane, 0)
 
 
 def zero_borders(ref):
@@ -126,7 +128,7 @@
         parts = []
         for q in range(BLOCK):
             x = block * BLOCK + q
-            base = (x - gap_x + MARGIN) * WIDE + MARGIN - gap_y
+            base = shifted_plane(x - gap_x) - gap_y
             for t in range(TILES):
                 value = shift[pl.ds(base + 8 * t, 8), :]
                 value = jnp.where(inside, pltpu.roll(value, turn, 1), 0.0)
@@ -177,7 +179,7 @@
     def back_block(block, _):
         for q in range(BLOCK):
             x = block * BLOCK + q
-            base = (x + gap_x + MARGIN) * WIDE + MARGIN + gap_y
+            base = shifted_plane(x + gap_x) + gap_y
             for t in range(TILES):
                 at = pl.ds(8 * t, 8)
                 value = shift[pl.ds(base + 8 * t, 8), :]
@@ -190,28 +192,37 @@
 
 REMOTE = 4
 QUOTA = 2
-
-
-def first_kernel(row, count, own, payload, note, sem):
+ROOM = 2
+
+
+def forward_box(box, target, buf, arrived, left):
+    planes = BOX_X // CHUNKS
+    pieces = [pl.ds(c * planes, planes) for c in range(CHUNKS)]
+    for c, at in enumerate(pieces):
+        pltpu.make_async_copy(box.at[at], buf.at[at], arrived.at[c]).start()
+    for c, at in enumerate(pieces):
+        pltpu.make_async_copy(box.at[at], buf.at[at], arrived.at[c]).wait()
+        pltpu.make_async_copy(buf.at[at], target.at[at], left.at[c]).start()
+    for c, at in enumerate(pieces):
+        pltpu.make_async_copy(buf.at[at], target.at[at], left.at[c]).wait()
+
+
+def first_kernel(row, count, own, payload, note, note_sem, buf, arrived, left):
     lane = lax.broadcasted_iota(jnp.int32, (8, BOX_Z), 1)
     value = jnp.where(lane == 2 * SLOTS, count[0].astype(F32), 0.0)
     for e in range(SLOTS):
         for k in range(2):
-            value = jnp.where(lane == 2 * e + k, row[0, e, k].astype(F32), value)
+            value = jnp.where(lane == 2 * e + k, row[0, k, e].astype(F32), value)
     note[...] = jnp.zeros_like(note)
     note[0:8, :] = value
-    box = pltpu.make_async_copy(own.at[0], payload.at[pl.ds(0, BOX_X)], sem.at[0])
-    extra = pltpu.make_async_copy(note, payload.at[BOX_X], sem.at[1])
-    box.start()
+    extra = pltpu.make_async_copy(note, payload.at[BOX_X], note_sem)
     extra.start()
-    box.wait()
+    forward_box(own.at[0], payload, buf, arrived, left)
     extra.wait()
 
 
-def second_kernel(own, box, sem):
-    copy = pltpu.make_async_copy(own.at[1], box, sem)
-    copy.start()
-    copy.wait()
+def second_kernel(own, target, buf, arrived, left):
+    forward_box(own.at[1], target, buf, arrived, left)
 
 
 def stage_kernel(stage, row, count, position, offsets, weights, values, own, mate, *rest):
@@ -220,10 +231,8 @@
     elif stage == 1:
         (payload, _, accum, leaving, *rest) = rest
         remote = payload.at[pl.ds(0, BOX_X)]
-    elif stage == 2:
-        (payload, remote, _, accum, leaving, *rest) = rest
     else:
-        (payload, _, accum, leaving, *rest) = rest
+        (payload, remote, _, accum, leaving, leaving_mate, *rest) = rest
     lead, shift, partner, one, two, three, work, note, sem, note_sem = rest
     here = position[0]
     mate_id = here ^ 1
@@ -236,7 +245,7 @@
         copy.wait()
 
     def near(e, k):
-        return row[0, e, k]
+        return row[0, k, e]
 
     def far(e, k):
         return note[0, 2 * e + k].astype(jnp.int32)
@@ -261,31 +270,35 @@
             for axis in range(3):
                 work[base + 2 + axis] = offsets[3 * partner_id + axis] - offsets[3 * lead_id + axis]
 
-    if stage in (0, 3):
-        seen = jnp.int32(0)
-        for e in range(SLOTS):
-            lead_id, partner_id = near(e, 0), near(e, 1)
-            inside = (
-                (e < count[0])
-                & (lead_id // ORB_DEV != across)
-                & (partner_id // ORB_DEV != across)
-            )
-            early = seen < QUOTA
-            push(inside & (early if stage == 0 else ~early), lead_id, partner_id)
-            seen = seen + inside.astype(jnp.int32)
-    if stage == 3:
+    inner = []
+    seen = jnp.int32(0)
+    for e in range(SLOTS):
+        lead_id, partner_id = near(e, 0), near(e, 1)
+        inside = (
+            (e < count[0])
+            & (lead_id // ORB_DEV != across)
+            & (partner_id // ORB_DEV != across)
+        )
+        inner.append((inside, seen - QUOTA, lead_id, partner_id))
+        seen = seen + inside.astype(jnp.int32)
+    if stage == 0:
+        for inside, order, lead_id, partner_id in inner:
+            push(inside & (order < 0), lead_id, partner_id)
+    else:
+        seen = jnp.maximum(seen - QUOTA, 0)
+        inner = [(inside & (order >= 0), order, a, b) for inside, order, a, b in inner]
         far_count = note[0, 2 * SLOTS].astype(jnp.int32)
         for e in range(SLOTS):
             lead_id, partner_id = far(e, 0), far(e, 1)
-            push(
+            inside = (
                 (e < far_count)
                 & (lead_id // ORB_DEV == here)
-                & (partner_id // ORB_DEV == here),
-                lead_id,
-                partner_id,
+                & (partner_id // ORB_DEV == here)
             )
-    if stage in (1, 2):
-        far_count = note[0, 2 * SLOTS].astype(jnp.int32)
+            inner.append((inside, seen, lead_id, partner_id))
+            seen = seen + inside.astype(jnp.int32)
+    if stage:
+        firsts = jnp.int32(0)
         left = jnp.where(is_left, here, across)
         right = jnp.where(is_left, across, here)
         entries = []
@@ -322,16 +335,20 @@
             at_right = (free & ~go_left) | (fixed if side == 1 else jnp.bool_(False))
             mine = (at_left & is_left) | (at_right & ~is_left)
             bit = jnp.where(is_left, right_bit, left_bit)
+            firsts = firsts + (mine & (bit == 0)).astype(jnp.int32)
             push(mine & (bit == stage - 1), a, b)
+        for inside, order, a, b in inner:
+            soon = order < ROOM - firsts
+            push(inside & (soon if stage == 1 else ~soon), a, b)
 
     total = work[0]
     sources = [own.at[0], own.at[1], mate.at[0], mate.at[1]]
-    if stage in (1, 2):
+    if stage:
         sources.append(remote)
 
     def window(buf):
         return shift.at[buf].reshape(SHIFT_PLANES, WIDE, BOX_Z).at[
-            pl.ds(MARGIN, BOX_X), pl.ds(MARGIN, BOX_Y), :
+            pl.ds(1, BOX_X), pl.ds(MARGIN, BOX_Y), :
         ]
 
     def fetch(k, buf):
@@ -376,14 +393,18 @@
     lax.fori_loop(0, total, visit, 0)
 
     if stage:
-        boxes = accum.at[pl.ds(2, 2)] if stage == 3 else accum.at[REMOTE]
-        copy = pltpu.make_async_copy(boxes, leaving, note_sem)
-        copy.start()
-        copy.wait()
-    if stage == 1:
-        @pl.when(total > 0)
-        def _():
-            zero_box(accum.at[REMOTE])
+        def leave(x, _):
+            for t in range(TILES):
+                at = pl.ds(8 * t, 8)
+                leaving[x, at, :] = accum[REMOTE, x, at, :]
+                if stage == 1:
+                    accum[REMOTE, x, at, :] = jnp.zeros((8, BOX_Z), F32)
+                else:
+                    for box in range(ORB_DEV):
+                        leaving_mate[box, x, at, :] = accum[2 + box, x, at, :]
+            return 0
+
+        lax.fori_loop(0, BOX_X, leave, 0, unroll=2)
 
 
 SMEM = pl.BlockSpec(memory_space=pltpu.SMEM)
@@ -398,8 +419,8 @@
     shapes = [jax.ShapeDtypeStruct((REMOTE + 1,) + BOX, F32)]
     outs = [VMEM]
     if stage:
-        shapes.append(jax.ShapeDtypeStruct(((2,) if stage == 3 else ()) + BOX, F32))
-        outs.append(VMEM)
+        shapes += [jax.ShapeDtypeStruct(shape + BOX, F32) for shape in ((), (2,))[:stage]]
+        outs += [VMEM] * stage
     return pl.pallas_call(
         functools.partial(stage_kernel, stage),
         out_shape=shapes,
@@ -422,7 +443,7 @@
         cost_estimate=pl.CostEstimate(
             flops=200_000_000, bytes_accessed=20_000_000, transcendentals=0
         ),
-        name="stage_" + "abcd"[stage],
+        name="stage_" + "abc"[stage],
     )(*operands)
 
 
@@ -440,38 +461,38 @@
     pltpu.make_async_copy(chunk, result.at[box], sem).wait()
 
 
-def run_total(box, accum, mate, remote, result=None):
-    operands = [accum, mate, remote]
-    specs = [VMEM, VMEM, VMEM]
-    aliases = {}
-    if result is not None:
-        operands.append(result)
-        specs.append(HBM)
-        aliases = {3: 0}
+def run_total(box, accum, mate, remote, result=()):
     return pl.pallas_call(
         functools.partial(total_kernel, box),
         out_shape=jax.ShapeDtypeStruct((ORB_DEV,) + BOX, F32),
-        in_specs=specs,
+        in_specs=[VMEM, VMEM, VMEM] + [HBM] * len(result),
         out_specs=HBM,
-        input_output_aliases=aliases,
+        input_output_aliases={3: 0} if result else {},
         scratch_shapes=[pltpu.VMEM(BOX, F32), pltpu.SemaphoreType.DMA],
         compiler_params=pltpu.CompilerParams(vmem_limit_bytes=4 << 20),
         name="total_" + "ab"[box],
-    )(*operands)
+    )(accum, mate, remote, *result)
 
 
 def local(orbitals, pair_list, pair_count, box_offset):
     position = lax.axis_index("orb").astype(jnp.int32)[None]
+    pair_list = jnp.transpose(pair_list, (0, 2, 1))
     devices = lax.axis_size("orb")
     mates = [(d, d ^ 1) for d in range(devices)]
     across = [(d, d + 1) for d in range(1, devices - 1, 2)]
     across = across + [(b, a) for a, b in across]
+    staging = [
+        pltpu.VMEM(BOX, F32),
+        pltpu.SemaphoreType.DMA((CHUNKS,)),
+        pltpu.SemaphoreType.DMA((CHUNKS,)),
+    ]
     payload = pl.pallas_call(
         first_kernel,
         out_shape=jax.ShapeDtypeStruct((BOX_X + 1, BOX_Y, BOX_Z), F32),
         in_specs=[SMEM, SMEM, HBM],
         out_specs=HBM,
-        scratch_shapes=[pltpu.VMEM((BOX_Y, BOX_Z), F32), pltpu.SemaphoreType.DMA((2,))],
+        scratch_shapes=[pltpu.VMEM((BOX_Y, BOX_Z), F32), pltpu.SemaphoreType.DMA] + staging,
+        compiler_params=pltpu.CompilerParams(vmem_limit_bytes=3 << 20),
         name="first_box",
     )(pair_list, pair_count, orbitals)
     payload, held = lax.optimization_barrier((payload, orbitals))
@@ -482,7 +503,8 @@
         out_shape=jax.ShapeDtypeStruct(BOX, F32),
         in_specs=[HBM],
         out_specs=HBM,
-        scratch_shapes=[pltpu.SemaphoreType.DMA],
+        scratch_shapes=staging,
+        compiler_params=pltpu.CompilerParams(vmem_limit_bytes=3 << 20),
         name="second_box",
     )(held)
     far_second = lax.ppermute(second, "orb", across)
@@ -494,13 +516,12 @@
     (accum,) = run_stage(0, fixed, (), None)
     accum, for_first = run_stage(1, fixed, (far_first,), accum)
     back_first = lax.ppermute(for_first, "orb", across)
-    accum, for_second = run_stage(2, fixed, (far_first, far_second), accum)
-    for_second, back_first, accum = lax.optimization_barrier((for_second, back_first, accum))
+    accum, for_second, for_mate = run_stage(2, fixed, (far_first, far_second), accum)
+    for_second, back_first = lax.optimization_barrier((for_second, back_first))
     back_second = lax.ppermute(for_second, "orb", across)
-    accum, for_mate = run_stage(3, fixed, (far_first,), accum)
     back_mate = lax.ppermute(for_mate, "orb", mates)
     result = run_total(0, accum, back_mate, back_first)
-    return run_total(1, accum, back_mate, back_second, result)
+    return run_total(1, accum, back_mate, back_second, (result,))
 
 
 def solution(mesh):

time: 208 us -> 101 us (0.49)
  the two profiles are of different devices: /device:TPU:80 before, /device:TPU:24 now
where the time goes in v2:
time: 101 us
  starting transfers between devices  40.2 us (40%)
  Pallas kernels  30 us (30%)
  waiting for transfers between devices  29.1 us (29%)
  local copies, waits for them, and re-layouts  1.04 us (1%)
    pallas_call x3, Pallas kernels, run_stage(): pl.pallas_call(functools.partial(stage_kernel, stage), out_shape=shapes,...  22.8 us
    ppermute x1, starting transfers between devices, local(): back_first = lax.ppermute(for_first, 'orb', across)  21.9 us
    ppermute x1, waiting for transfers between devices, local(): back_second = lax.ppermute(for_second, 'orb', across)  16.9 us
    ppermute x1, starting transfers between devices, local(): far_first = lax.ppermute(payload, 'orb', across)  8.41 us
    ppermute x1, starting transfers between devices, local(): back_second = lax.ppermute(for_second, 'orb', across)  7.85 us
    ppermute x1, waiting for transfers between devices, local(): back_first = lax.ppermute(for_first, 'orb', across)  7.12 us
    ppermute x1, waiting for transfers between devices, local(): far_first = lax.ppermute(payload, 'orb', across)  5.06 us
    pallas_call x1, Pallas kernels, local(): pl.pallas_call(first_kernel, out_shape=jax.ShapeDtypeStruct((BOX_X + 1, B...  2.76 us
  transfers between devices with their start and end apart: 6, of which 3 were waited for; matrix products, arithmetic and copies ran while one was open for 0% of the time, Pallas kernels for 26%

profile of v2, /device:TPU:24, one launch (start us, length us, event | category | flops | bytes accessed | tf_op | source)
XLA Modules:
  0.0 101.2 jit_solution(9444680865979289860)
XLA Ops:
  0.7 0.0 copy-start.2
  0.7 0.7 copy-done.2
  1.3 2.8 %first_box.1 = f32[49,64,128]{2,1,0:T(8,128)} custom-call(s32[1,2,6]{2,1,0:T(2,128)S(1)} %bitcast.2, s32[1]{0:T(128)S(6)} %copy.14.count, f32[2,48,64,128]{3,2,1,0:T(8,128)} %own.8), custom_call_target="tpu_custom_call" | custom-call | tf_op jit(solution)/shard_map/first_box/pallas_call | solution.py:489
  4.1 0.0 copy-start.4
  4.1 0.0 copy-start
  4.1 0.0 copy-start.1
  4.1 0.0 copy-start.3
  4.1 0.1 collective-permute-start
  4.2 8.4 %collective-permute-start.1 = (f32[49,64,128]{2,1,0:T(8,128)}, f32[49,64,128]{2,1,0:T(8,128)}, u32[]{:S(2)}, u32[]{:S(2)}) collective-permute-start(f32[49,64,128]{2,1,0:T(8,128)} %first_box.1), channel_id=1, source_target_pairs={{1,2},{3,4},{5,6},{7,8},{9,10},{11,12},{13,14},{15,16},{17,18},{19... | collective-permute-start | bytes 4816904 | tf_op jit(solution)/shard_map/ppermute | solution.py:499
  12.7 2.2 %second_box.1 = f32[48,64,128]{2,1,0:T(8,128)} custom-call(f32[2,48,64,128]{3,2,1,0:T(8,128)} %own.8), custom_call_target="tpu_custom_call" | custom-call | tf_op jit(solution)/shard_map/second_box/pallas_call | solution.py:501
  14.9 1.9 %collective-permute-start.2 = (f32[48,64,128]{2,1,0:T(8,128)}, f32[48,64,128]{2,1,0:T(8,128)}, u32[]{:S(2)}, u32[]{:S(2)}) collective-permute-start(f32[48,64,128]{2,1,0:T(8,128)} %second_box.1), channel_id=1, source_target_pairs={{1,2},{3,4},{5,6},{7,8},{9,10},{11,12},{13,14},{15,16},{17,18},{19... | collective-permute-start | bytes 4718600 | tf_op jit(solution)/shard_map/ppermute | solution.py:510
  16.8 0.1 copy.10
  17.0 0.2 reshape.3.offsets
  17.2 9.1 %stage_a.1.rest_1_ = f32[5,48,64,128]{3,2,1,0:T(8,128)S(1)} custom-call(s32[1,2,6]{2,1,0:T(2,128)S(1)} %bitcast.3, s32[1]{0:T(128)S(6)} %copy.14.count, s32[1]{0:T(128)} %bitcast.1.position, s32[768]{0:T(1024)S(1)} %reshape.3.offsets, bf16[256,256]{1,0:T(8,128)(2,1)S(1)} %copy-done, f32[8,128]{1,0:T(8,128)S(1)} %copy-done.1, f32[2,48,64,128]{3,2,1,0:T(8,128)} %own.8, ...), custom_call_target="tpu_custom_call" | custom-call | flops 200000000 | bytes 20000000 | tf_op jit(solution)/shard_map/stage_a/pallas_call | solution.py:424
  26.4 5.1 %collective-permute-done.1.rest_0_ = f32[49,64,128]{2,1,0:T(8,128)} collective-permute-done((f32[49,64,128]{2,1,0:T(8,128)}, f32[49,64,128]{2,1,0:T(8,128)}, u32[]{:S(2)}, u32[]{:S(2)}) %collective-permute-start.1) | collective-permute-done | bytes 1605664 | tf_op jit(solution)/shard_map/ppermute | solution.py:499
  31.4 2.8 %stage_b.1 = (f32[5,48,64,128]{3,2,1,0:T(8,128)S(1)}, f32[48,64,128]{2,1,0:T(8,128)S(1)}) custom-call(s32[1,2,6]{2,1,0:T(2,128)S(1)} %bitcast.4, s32[1]{0:T(128)S(6)} %copy.14.count, s32[1]{0:T(128)} %bitcast.1.position, s32[768]{0:T(1024)S(1)} %reshape.3.offsets, bf16[256,256]{1,0:T(8,128)(2,1)S(1)} %copy-done, ...), custom_call_target="tpu_custom_call", output_to_operand_aliasing={{0}: (9, {})} | custom-call | flops 200000000 | bytes 20000000 | tf_op jit(solution)/shard_map/stage_b/pallas_call | solution.py:424
  34.2 21.9 %collective-permute-start.4 = (f32[48,64,128]{2,1,0:T(8,128)S(1)}, f32[48,64,128]{2,1,0:T(8,128)S(1)}, u32[]{:S(2)}, u32[]{:S(2)}) collective-permute-start(f32[48,64,128]{2,1,0:T(8,128)S(1)} %get-tuple-element.20), channel_id=1, source_target_pairs={{1,2},{3,4},{5,6},{7,8},{9,10},{11,12},{13,14},{15,16},{17,18},{19... | collective-permute-start | bytes 4718600 | tf_op jit(solution)/shard_map/ppermute | solution.py:518
  56.1 10.9 %stage_c.1 = (f32[5,48,64,128]{3,2,1,0:T(8,128)S(1)}, f32[48,64,128]{2,1,0:T(8,128)S(1)}, f32[2,48,64,128]{3,2,1,0:T(8,128)S(1)}) custom-call(s32[1,2,6]{2,1,0:T(2,128)S(1)} %bitcast.5, s32[1]{0:T(128)S(6)} %copy.14.count, s32[1]{0:T(128)} %bitcast.1.position, s32[768]{0:T(1024)S(1)} %reshape.3.offsets, ...), custom_call_target="tpu_custom_call", output_to_operand_aliasing={{0}: (10, {})} | custom-call | flops 200000000 | bytes 20000000 | tf_op jit(solution)/shard_map/stage_c/pallas_call | solution.py:424
  66.9 0.1 collective-permute-start.3
  67.0 7.1 %collective-permute-done.4.remote = f32[48,64,128]{2,1,0:T(8,128)S(1)} collective-permute-done((f32[48,64,128]{2,1,0:T(8,128)S(1)}, f32[48,64,128]{2,1,0:T(8,128)S(1)}, u32[]{:S(2)}, u32[]{:S(2)}) %collective-permute-start.4) | collective-permute-done | bytes 1572896 | tf_op jit(solution)/shard_map/ppermute | solution.py:518
  74.2 7.8 %collective-permute-start.5 = (f32[48,64,128]{2,1,0:T(8,128)S(1)}, f32[48,64,128]{2,1,0:T(8,128)S(1)}, u32[]{:S(2)}, u32[]{:S(2)}) collective-permute-start(f32[48,64,128]{2,1,0:T(8,128)S(1)} %get-tuple-element.21), channel_id=1, source_target_pairs={{1,2},{3,4},{5,6},{7,8},{9,10},{11,12},{13,14},{15,16},{17,18},{19... | collective-permute-start | bytes 4718600 | tf_op jit(solution)/shard_map/ppermute | solution.py:521
  82.0 1.1 %total_a.1.rest_0_ = f32[2,48,64,128]{3,2,1,0:T(8,128)} custom-call(f32[5,48,64,128]{3,2,1,0:T(8,128)S(1)} %get-tuple-element.17.accum, f32[2,48,64,128]{3,2,1,0:T(8,128)S(1)} %collective-permute-done.3.mate, f32[48,64,128]{2,1,0:T(8,128)S(1)} %collective-permute-done.4.remote), custom_call_target="tpu_custom_call" | custom-call | tf_op jit(solution)/shard_map/total_a/pallas_call | solution.py:465
  83.2 16.9 %collective-permute-done.5.remote = f32[48,64,128]{2,1,0:T(8,128)S(1)} collective-permute-done((f32[48,64,128]{2,1,0:T(8,128)S(1)}, f32[48,64,128]{2,1,0:T(8,128)S(1)}, u32[]{:S(2)}, u32[]{:S(2)}) %collective-permute-start.5) | collective-permute-done | bytes 1572896 | tf_op jit(solution)/shard_map/ppermute | solution.py:521
  100.1 1.1 %total_b.1 = f32[2,48,64,128]{3,2,1,0:T(8,128)} custom-call(f32[5,48,64,128]{3,2,1,0:T(8,128)S(1)} %get-tuple-element.17.accum, f32[2,48,64,128]{3,2,1,0:T(8,128)S(1)} %collective-permute-done.3.mate, f32[48,64,128]{2,1,0:T(8,128)S(1)} %collective-permute-done.5.remote, f32[2,48,64,128]{3,2,1,0:T(8,128)} %total_a.1.rest_0_), custom_call_target="tpu_custom_call", output_to_operand_aliasing={{}: (3, {})} | custom-call | tf_op jit(solution)/shard_map/total_b/pallas_call | solution.py:465
  (7 shorter events, 0.0 us)
Async XLA Ops:
  0.7 0.7 copy-start.2
  4.1 12.7 %copy-start.4 = (s32[256,3]{0,1:T(4,128)S(1)}, s32[256,3]{0,1:T(4,128)}, u32[]{:S(2)}) copy-start(s32[256,3]{0,1:T(4,128)} %param.9) | copy-start | bytes 9220
  4.1 13.1 %copy-start = (bf16[256,256]{1,0:T(8,128)(2,1)S(1)}, bf16[256,256]{1,0:T(8,128)(2,1)}, u32[]{:S(2)}) copy-start(bf16[256,256]{1,0:T(8,128)(2,1)} %constant.8.clone.weights) | copy-start | bytes 393220
  4.1 13.1 %copy-start.1 = (f32[8,128]{1,0:T(8,128)S(1)}, f32[8,128]{1,0:T(8,128)}, u32[]{:S(2)}) copy-start(f32[8,128]{1,0:T(8,128)} %constant.9.clone.values) | copy-start | bytes 12292
  4.1 13.1 %copy-start.3 = (s32[1,6,2]{1,2,0:T(2,128)S(1)}, s32[1,6,2]{1,2,0:T(2,128)}, u32[]{:S(2)}) copy-start(s32[1,6,2]{1,2,0:T(2,128)} %param.7) | copy-start | bytes 148
  4.1 13.0 %collective-permute-start = (f32[2,48,64,128]{3,2,1,0:T(8,128)}, f32[2,48,64,128]{3,2,1,0:T(8,128)S(1)}, u32[]{:S(2)}, u32[]{:S(2)}) collective-permute-start(f32[2,48,64,128]{3,2,1,0:T(8,128)} %own.8), channel_id=1, source_target_pairs={{0,1},{1,0},{2,3},{3,2},{4,5},{5,4},{6,7},{7,6},{8,9},{9,8},{10,11... | collective-permute-start | bytes 9437192 | tf_op jit(solution)/shard_map/ppermute | solution.py:500
  4.2 27.2 %collective-permute-start.1 = (f32[49,64,128]{2,1,0:T(8,128)}, f32[49,64,128]{2,1,0:T(8,128)}, u32[]{:S(2)}, u32[]{:S(2)}) collective-permute-start(f32[49,64,128]{2,1,0:T(8,128)} %first_box.1), channel_id=1, source_target_pairs={{1,2},{3,4},{5,6},{7,8},{9,10},{11,12},{13,14},{15,16},{17,18},{19... | collective-permute-start | bytes 4816904 | tf_op jit(solution)/shard_map/ppermute | solution.py:499
  14.9 41.2 %collective-permute-start.2 = (f32[48,64,128]{2,1,0:T(8,128)}, f32[48,64,128]{2,1,0:T(8,128)}, u32[]{:S(2)}, u32[]{:S(2)}) collective-permute-start(f32[48,64,128]{2,1,0:T(8,128)} %second_box.1), channel_id=1, source_target_pairs={{1,2},{3,4},{5,6},{7,8},{9,10},{11,12},{13,14},{15,16},{17,18},{19... | collective-permute-start | bytes 4718600 | tf_op jit(solution)/shard_map/ppermute | solution.py:510
  34.2 39.9 %collective-permute-start.4 = (f32[48,64,128]{2,1,0:T(8,128)S(1)}, f32[48,64,128]{2,1,0:T(8,128)S(1)}, u32[]{:S(2)}, u32[]{:S(2)}) collective-permute-start(f32[48,64,128]{2,1,0:T(8,128)S(1)} %get-tuple-element.20), channel_id=1, source_target_pairs={{1,2},{3,4},{5,6},{7,8},{9,10},{11,12},{13,14},{15,16},{17,18},{19... | collective-permute-start | bytes 4718600 | tf_op jit(solution)/shard_map/ppermute | solution.py:518
  66.9 15.1 %collective-permute-start.3 = (f32[2,48,64,128]{3,2,1,0:T(8,128)S(1)}, f32[2,48,64,128]{3,2,1,0:T(8,128)S(1)}, u32[]{:S(2)}, u32[]{:S(2)}) collective-permute-start(f32[2,48,64,128]{3,2,1,0:T(8,128)S(1)} %get-tuple-element.18), channel_id=1, source_target_pairs={{0,1},{1,0},{2,3},{3,2},{4,5},{5,4},{6,7},{7,6},{8,9},{9,8},{10,11... | collective-permute-start | bytes 9437192 | tf_op jit(solution)/shard_map/ppermute | solution.py:522
  74.2 25.9 %collective-permute-start.5 = (f32[48,64,128]{2,1,0:T(8,128)S(1)}, f32[48,64,128]{2,1,0:T(8,128)S(1)}, u32[]{:S(2)}, u32[]{:S(2)}) collective-permute-start(f32[48,64,128]{2,1,0:T(8,128)S(1)} %get-tuple-element.21), channel_id=1, source_target_pairs={{1,2},{3,4},{5,6},{7,8},{9,10},{11,12},{13,14},{15,16},{17,18},{19... | collective-permute-start | bytes 4718600 | tf_op jit(solution)/shard_map/ppermute | solution.py:521
